TPU v7x, 256 devices: a whole 4x4x8 slice. The times are simulated.
256 devices in a mesh: seq: 8 (over y, z_lo), exp: 32 (over x, z_hi, core).
Axes of the slice: x: 4, y: 4, z: 8 (z_hi: 4, z_lo: 2; z = z_hi * 2 + z_lo), core: 2. Of those that a mesh axis runs over, the one named last changes fastest.
Arguments:
- tokens: bfloat16 [16384, 4096], P(('seq', 'exp')), may hold values from -6 to 6
- norm_gain: float32 [4096], replicated, may hold values from 0.1 to 1.9
- queries: bfloat16 [16384, 2048], P(('seq', 'exp')), may hold values from -24 to 24
- attn_keys: bfloat16 [16384, 2048], P(('seq', 'exp')), may hold values from -4.5 to 4.5
- attn_values: bfloat16 [16384, 2048], P(('seq', 'exp')), may hold values from -6 to 6
- expert_ids: int32 [16384, 2], P(('seq', 'exp')), may hold values from 0 to 63, all different within a row; in each aligned block of 64 rows (0 to 63, 64 to 127, ...) at most 2 rows name the same one
- route_weights: float32 [16384, 2], P(('seq', 'exp')), may hold values from 0.1 to 1
- gate_proj: bfloat16 [64, 1408, 4096], P('exp', 'seq'), may hold values from -0.09375 to 0.09375
- up_proj: bfloat16 [64, 1408, 4096], P('exp', 'seq'), may hold values from -0.09375 to 0.09375
- down_proj: bfloat16 [64, 1408, 4096], P('exp', 'seq'), may hold values from -0.15625 to 0.15625
Outputs:
- attention: bfloat16 [16384, 2048], P(('seq', 'exp'))
- expert_mix: bfloat16 [16384, 4096], P(('seq', 'exp'))
Inputs may be any that keep to these rules, and one draw needn't show every extreme that they name: `expert_ids`: the two experts of a token differ. Among the rows of one device (64 consecutive tokens, aligned), every expert is named exactly 2 times.
All inputs are finite; a program needn't handle non-finite values.
Results may differ from a plain program's by a relative error of at most 0.015.
Values may be sent and summed in bfloat16 or wider, within the bound.
A program may use at most 128 MiB of HBM per device.

v0:
```python
import math

import jax
import jax.numpy as jnp
from jax import lax
from jax.sharding import PartitionSpec as P

EXPERTS = 64
HDIM = 64
SUMS = 64
SEG_DEV = 2
CAP = 2


EPS = 1e-05
NEG = -1e30


def broadcast(value, axis, source):
    kept = jnp.where(lax.axis_index(axis) == source, value, 0).astype(value.dtype)
    return lax.psum(kept, axis)


def normalize(tokens, norm_gain):
    values = tokens.astype(jnp.float32)
    inv_rms = lax.rsqrt(jnp.mean(values * values, axis=-1, keepdims=True) + EPS)
    return (values * inv_rms * norm_gain).astype(jnp.bfloat16)


def attend_block(
    query_blk, seg_keys, seg_values, sum_keys, sum_values, first_row, segment, score_scale
):
    local_sc = (
        jnp.einsum("qhd,khd->hqk", query_blk, seg_keys, preferred_element_type=jnp.float32)
        * score_scale
    )
    summ_sc = (
        jnp.einsum("qhd,khd->hqk", query_blk, sum_keys, preferred_element_type=jnp.float32)
        * score_scale
    )
    query_pos = first_row + jnp.arange(query_blk.shape[0], dtype=jnp.int32)
    key_pos = jnp.arange(seg_keys.shape[0], dtype=jnp.int32)
    local_ok = key_pos[None, :] <= query_pos[:, None]
    summ_ok = jnp.arange(sum_keys.shape[0], dtype=jnp.int32) // SUMS < segment
    local_sc = jnp.where(local_ok[None], local_sc, NEG)
    summ_sc = jnp.where(summ_ok[None, None], summ_sc, NEG)
    top_sc = jnp.maximum(
        jnp.max(local_sc, axis=-1, keepdims=True), jnp.max(summ_sc, axis=-1, keepdims=True)
    )
    local_ex = jnp.exp(local_sc - top_sc)
    summ_ex = jnp.exp(summ_sc - top_sc)
    totals = jnp.sum(local_ex, axis=-1, keepdims=True) + jnp.sum(summ_ex, axis=-1, keepdims=True)
    local_wt = (local_ex / totals).astype(jnp.bfloat16)
    summ_wt = (summ_ex / totals).astype(jnp.bfloat16)
    mixed_out = jnp.einsum("hqk,khd->qhd", local_wt, seg_values, preferred_element_type=jnp.float32)
    return mixed_out + jnp.einsum(
        "hqk,khd->qhd", summ_wt, sum_values, preferred_element_type=jnp.float32
    )


def slot_table(id_rows):
    onehot = (id_rows[..., None] == jnp.arange(EXPERTS, dtype=jnp.int32)).astype(jnp.int32)
    before = jnp.cumsum(onehot, axis=-2) - onehot
    return jnp.sum(before * onehot, axis=-1)


def fill_slots(rows, slot_pos, slot_total):
    row_count = rows.shape[0]
    padded = jnp.concatenate([rows, jnp.zeros((1, rows.shape[1]), rows.dtype)], axis=0)
    source_row = jnp.arange(row_count * 2, dtype=jnp.int32) // 2
    index_table = jnp.full((slot_total,), row_count, jnp.int32).at[slot_pos].set(source_row)
    return padded[index_table]


def expert_block(row_block, gate_proj, up_proj, down_proj):
    gate_act = jnp.einsum(
        "...ecd,efd->...ecf", row_block, gate_proj, preferred_element_type=jnp.float32
    )
    up_act = jnp.einsum(
        "...ecd,efd->...ecf", row_block, up_proj, preferred_element_type=jnp.float32
    )
    hidden = (jax.nn.silu(gate_act) * up_act).astype(jnp.bfloat16)
    return jnp.einsum("...ecf,efd->...ecd", hidden, down_proj, preferred_element_type=jnp.float32)


def on_device(
    tokens,
    norm_gain,
    queries,
    attn_keys,
    attn_values,
    expert_ids,
    route_weights,
    gate_proj,
    up_proj,
    down_proj,
):
    exp_count = lax.axis_size("exp")
    seq_count = lax.axis_size("seq")
    local_tokens = tokens.shape[0]
    feature_count = tokens.shape[1]
    normed = normalize(tokens, norm_gain)
    head_q, head_k, head_v = (
        lax.all_to_all(queries, "exp", split_axis=1, concat_axis=0, tiled=True),
        lax.all_to_all(attn_keys, "exp", split_axis=1, concat_axis=0, tiled=True),
        lax.all_to_all(attn_values, "exp", split_axis=1, concat_axis=0, tiled=True),
    )
    heads_dev = head_q.shape[1] // HDIM
    seg_len = head_q.shape[0] // SEG_DEV
    block_len = seg_len // SUMS
    head_q = head_q.reshape(SEG_DEV, seg_len, heads_dev, HDIM)
    head_k = head_k.reshape(SEG_DEV, seg_len, heads_dev, HDIM)
    head_v = head_v.reshape(SEG_DEV, seg_len, heads_dev, HDIM)
    inv_block = 1.0 / math.sqrt(block_len)
    sum_k = (
        jnp.sum(
            head_k.astype(jnp.float32).reshape(SEG_DEV, SUMS, block_len, heads_dev, HDIM), axis=2
        )
        * inv_block
    ).astype(jnp.bfloat16)
    sum_v = (
        jnp.sum(
            head_v.astype(jnp.float32).reshape(SEG_DEV, SUMS, block_len, heads_dev, HDIM), axis=2
        )
        * inv_block
    ).astype(jnp.bfloat16)
    sum_k = sum_k.reshape(SEG_DEV * SUMS, heads_dev, HDIM)
    sum_v = sum_v.reshape(SEG_DEV * SUMS, heads_dev, HDIM)
    key_list = []
    value_list = []
    for root_index in range(seq_count):
        recv_keys, recv_values = (
            broadcast(sum_k, "seq", root_index),
            broadcast(sum_v, "seq", root_index),
        )
        key_list.append(recv_keys)
        value_list.append(recv_values)
    all_keys = jnp.concatenate(key_list, axis=0)
    all_values = jnp.concatenate(value_list, axis=0)
    query_rows = min(512, seg_len)
    score_scale = 1.0 / math.sqrt(HDIM)
    seg_base = lax.axis_index("seq") * SEG_DEV
    pieces = []
    for local_seg in range(SEG_DEV):
        for first_row in range(0, seg_len, query_rows):
            block_out = attend_block(
                head_q[local_seg, first_row : first_row + query_rows],
                head_k[local_seg],
                head_v[local_seg],
                all_keys,
                all_values,
                first_row,
                seg_base + local_seg,
                score_scale,
            )
            pieces.append(block_out.astype(jnp.bfloat16))
    head_out = jnp.concatenate(pieces, axis=0).reshape(SEG_DEV * seg_len, heads_dev * HDIM)
    attention = lax.all_to_all(head_out, "exp", split_axis=0, concat_axis=1, tiled=True)
    exp_dev = EXPERTS // exp_count
    flat_ids = expert_ids.reshape(-1)
    local_pos = flat_ids * CAP + slot_table(flat_ids)
    group_normed, group_ids = (
        lax.all_gather(normed, "seq", axis=0, tiled=True),
        lax.all_gather(expert_ids, "seq", axis=0, tiled=True),
    )
    id_rows = group_ids.reshape(seq_count, local_tokens * 2)
    slot_ids = slot_table(id_rows)
    source_ids = jnp.arange(seq_count, dtype=jnp.int32)[:, None]
    owner_dev = id_rows // exp_dev
    within = id_rows % exp_dev
    slot_pos = ((owner_dev * seq_count + source_ids) * exp_dev + within) * CAP + slot_ids
    send_rows = fill_slots(group_normed, slot_pos.reshape(-1), EXPERTS * seq_count * CAP)
    send_rows = send_rows.reshape(exp_count, seq_count, exp_dev, CAP, feature_count)
    recv_rows = lax.all_to_all(send_rows, "exp", split_axis=0, concat_axis=0, tiled=True)
    slice_term = expert_block(recv_rows, gate_proj, up_proj, down_proj)
    summed = lax.psum_scatter(
        slice_term.astype(jnp.bfloat16), "seq", scatter_dimension=1, tiled=True
    )
    owner_out = summed.reshape(exp_count, exp_dev * CAP, feature_count)
    source_out = lax.all_to_all(owner_out, "exp", split_axis=0, concat_axis=0, tiled=True).reshape(
        EXPERTS * CAP, feature_count
    )
    picked = source_out[local_pos].astype(jnp.float32).reshape(local_tokens, 2, feature_count)
    expert_mix = jnp.sum(route_weights[:, :, None] * picked, axis=1).astype(jnp.bfloat16)
    return (attention, expert_mix)


def solution(mesh):
    return jax.shard_map(
        on_device,
        mesh=mesh,
        in_specs=(
            P(("seq", "exp"), None),
            P(),
            P(("seq", "exp"), None),
            P(("seq", "exp"), None),
            P(("seq", "exp"), None),
            P(("seq", "exp"), None),
            P(("seq", "exp"), None),
            P("exp", "seq", None),
            P("exp", "seq", None),
            P("exp", "seq", None),
        ),
        out_specs=(P(("seq", "exp"), None), P(("seq", "exp"), None)),
        check_vma=False,
    )
```

profile of v0, /device:TPU:1, one launch (start us, length us, event | category | flops | bytes accessed | tf_op | source)
XLA Modules:
  0.0 653.5 jit_solution(4916319611330004537)
XLA Ops:
  7.2 1.4 fusion.51
  8.7 2.0 fusion.53
  10.7 1.3 all_to_all.62
  12.1 1.2 copy.142
  13.3 1.1 reshape.872
  14.4 12.6 %all-to-all-start.2 = ((bf16[32,2,2048]{2,1,0:T(2,128)(2,1)}), bf16[32,2,2048]{2,1,0:T(2,128)(2,1)}, u32[]{:S(2)}, u32[]{:S(2)}) async-start(bf16[32,2,2048]{2,1,0:T(2,128)(2,1)} %reshape.872), calls=%async_computation.2 | async-start | bytes 524288 | tf_op jit(solution)/shard_map/all_to_all | solution.py:106
  27.1 20.9 %all-gather = s32[8,64,2]{1,2,0:T(2,128)S(1)} all-gather(s32[1,64,2]{1,2,0:T(2,128)S(1)} %bitcast.256), channel_id=1, replica_groups=mesh['seq'=8,'exp'=32] {'seq'}, dimensions={0}, use_global_device_ids=true | all-gather | bytes 4608 | tf_op jit(solution)/shard_map/all_gather | solution.py:164
  49.0 2.3 all_to_all.59
  51.2 1.2 copy.143
  52.5 1.1 reshape.868
  53.6 1.1 reshape.827
  54.7 2.5 select_reduce_fusion
  57.3 11.8 %all-to-all-start.1 = ((bf16[32,2,2048]{2,1,0:T(2,128)(2,1)}), bf16[32,2,2048]{2,1,0:T(2,128)(2,1)S(1)}, u32[]{:S(2)}, u32[]{:S(2)}) async-start(bf16[32,2,2048]{2,1,0:T(2,128)(2,1)} %reshape.868), calls=%async_computation.1 | async-start | bytes 524288 | tf_op jit(solution)/shard_map/all_to_all | solution.py:105
  69.1 4.3 scatter_custom_fusion
  73.5 45.5 %all-gather.3.cloned.1.call-done = bf16[512,4096]{1,0:T(8,128)(2,1)} async-done(((bf16[64,4096]{1,0:T(8,128)(2,1)}), bf16[512,4096]{1,0:T(8,128)(2,1)}) %all-gather.3.cloned.1.call-update) | async-done | bytes 4194320 | tf_op jit(solution)/shard_map/all_gather | solution.py:163
  119.0 4.7 concatenate.15
  123.7 17.8 %gather_fusion = bf16[1024,4096]{1,0:T(8,128)(2,1)} fusion(bf16[513,4096]{1,0:T(8,128)(2,1)} %concatenate.15, s32[1024]{0:T(1024)S(1)} %fusion.100), kind=kCustom, calls=%fused_computation | custom fusion | bytes 16781312 | tf_op jit(solution)/shard_map/gather | solution.py:72
  141.5 14.3 %reshape.828 = bf16[32,8,2,2,4096]{4,3,2,1,0:T(2,128)(2,1)} reshape(bf16[1024,4096]{1,0:T(8,128)(2,1)} %gather_fusion) | data formatting | bytes 16777216 | tf_op jit(solution)/shard_map/reshape | solution.py:173
  155.8 16.3 %copy.59 = bf16[32,8,2,2,4096]{4,1,3,2,0:T(8,128)(2,1)} copy(bf16[32,8,2,2,4096]{4,3,2,1,0:T(2,128)(2,1)} %reshape.828) | data formatting | bytes 16777216 | tf_op jit(solution)/shard_map/reshape | solution.py:173
  172.9 9.9 %all-to-all-start.4 = ((bf16[32,8,2,2,4096]{4,1,3,2,0:T(8,128)(2,1)}), bf16[32,8,2,2,4096]{4,1,3,2,0:T(8,128)(2,1)}, u32[]{:S(2)}, u32[]{:S(2)}) async-start(bf16[32,8,2,2,4096]{4,1,3,2,0:T(8,128)(2,1)} %copy.59), calls=%async_computation.4 | async-start | bytes 16777216 | tf_op jit(solution)/shard_map/all_to_all | solution.py:174
  182.8 1.3 reshape.873
  184.2 2.1 reshape.869
  186.5 1.3 convert_reduce_fusion.1
  190.3 198.7 %all-to-all-done.4 = bf16[32,8,2,2,4096]{4,1,3,2,0:T(8,128)(2,1)} async-done(((bf16[32,8,2,2,4096]{4,1,3,2,0:T(8,128)(2,1)}), bf16[32,8,2,2,4096]{4,1,3,2,0:T(8,128)(2,1)}, u32[]{:S(2)}, u32[]{:S(2)}) %all-to-all-start.4) | async-done | bytes 8388640 | tf_op jit(solution)/shard_map/all_to_all | solution.py:174
  389.0 6.7 %fusion.19 = f32[32,8,2,2,176]{4,1,3,0,2:T(8,128)S(1)} fusion(bf16[2,176,4096]{2,1,0:T(8,128)(2,1)} %param.17, bf16[32,8,2,2,4096]{4,1,3,2,0:T(8,128)(2,1)} %all-to-all-done.4), kind=kOutput, calls=%fused_computation.50 | convolution fusion | flops 1476395008 | bytes 11993088 | tf_op jit(solution)/shard_map/...ecd,efd->...ecf/dot_general | solution.py:76
  395.7 6.0 fusion.34
  401.8 5.5 convert_bitcast_fusion
  407.3 11.4 %copy.62 = bf16[32,8,2,2,4096]{4,0,3,2,1:T(8,128)(2,1)} copy(bf16[32,8,2,2,4096]{4,1,3,0,2:T(8,128)(2,1)} %convert_bitcast_fusion) | data formatting | bytes 16777216 | tf_op jit(solution)/shard_map/convert_element_type | solution.py:177
  418.7 0.9 copy-done.9
  419.9 1.1 reshape.870
  421.0 4.9 all-to-all-start
  426.0 15.7 %all-to-all-done = bf16[32,2,2048]{2,1,0:T(2,128)(2,1)S(1)} async-done(((bf16[32,2,2048]{2,1,0:T(2,128)(2,1)}), bf16[32,2,2048]{2,1,0:T(2,128)(2,1)S(1)}, u32[]{:S(2)}, u32[]{:S(2)}) %all-to-all-start) | async-done | bytes 262176 | tf_op jit(solution)/shard_map/all_to_all | solution.py:104
  443.3 1.9 fusion.118
  445.2 1.9 fusion.116
  447.1 1.9 fusion.117
  449.0 1.9 fusion.115
  450.9 0.9 constant_dynamic-update-slice_fusion.7
  469.4 1.0 fusion.57
  471.8 1.1 reshape.874
  472.9 5.2 all-to-all-start.3
  478.1 119.9 %reduce-scatter.2.cloned.1.call-done = bf16[32,1,2,2,4096]{4,0,3,2,1:T(8,128)(2,1)} async-done(((bf16[32,8,2,2,4096]{4,0,3,2,1:T(8,128)(2,1)}), bf16[32,1,2,2,4096]{4,0,3,2,1:T(8,128)(2,1)}) %reduce-scatter.2.cloned.1.call-update) | async-done | bytes 1048592 | tf_op jit(solution)/shard_map/reduce_scatter | solution.py:176
  598.0 3.0 copy.63
  601.0 9.2 %all-to-all-start.5 = ((bf16[32,4,4096]{2,1,0:T(4,128)(2,1)}), bf16[32,4,4096]{2,1,0:T(4,128)(2,1)S(1)}, u32[]{:S(2)}, u32[]{:S(2)}) async-start(bf16[32,4,4096]{2,1,0:T(4,128)(2,1)} %copy.63), calls=%async_computation.6 | async-start | bytes 2097152 | tf_op jit(solution)/shard_map/all_to_all | solution.py:180
  611.7 0.9 copy.66
  612.6 22.6 %all-to-all-done.5 = bf16[32,4,4096]{2,1,0:T(4,128)(2,1)S(1)} async-done(((bf16[32,4,4096]{2,1,0:T(4,128)(2,1)}), bf16[32,4,4096]{2,1,0:T(4,128)(2,1)S(1)}, u32[]{:S(2)}, u32[]{:S(2)}) %all-to-all-start.5) | async-done | bytes 1048608 | tf_op jit(solution)/shard_map/all_to_all | solution.py:180
  635.4 2.2 gather_fusion.1
  637.6 3.5 reshape.833
  641.2 5.6 multiply_reduce_fusion
  (136 shorter events, 26.9 us)
Async XLA Ops:
  7.2 394.6 %copy-start = (bf16[2,176,4096]{2,1,0:T(8,128)(2,1)S(1)}, bf16[2,176,4096]{2,1,0:T(8,128)(2,1)}, u32[]{:S(2)}) copy-start(bf16[2,176,4096]{2,1,0:T(8,128)(2,1)} %param.19) | copy-start | bytes 8650756
  7.2 3.6 copy-start.8
  7.2 111.8 %all-gather.3.cloned.1.call-start = ((), (), s32[]{:S(2)}) async-start(), calls=%async_computation.7 | async-start | bytes 4718592 | tf_op jit(solution)/shard_map/all_gather | solution.py:163
  10.7 16.3 %copy-start.20 = (s32[64,2]{0,1:T(2,128)S(1)}, s32[64,2]{0,1:T(2,128)}, u32[]{:S(2)}) copy-start(s32[64,2]{0,1:T(2,128)} %param.15) | copy-start | bytes 1540
  14.4 42.9 %all-to-all-start.2 = ((bf16[32,2,2048]{2,1,0:T(2,128)(2,1)}), bf16[32,2,2048]{2,1,0:T(2,128)(2,1)}, u32[]{:S(2)}, u32[]{:S(2)}) async-start(bf16[32,2,2048]{2,1,0:T(2,128)(2,1)} %reshape.872), calls=%async_computation.2 | async-start | bytes 524288 | tf_op jit(solution)/shard_map/all_to_all | solution.py:106
  57.3 114.8 %all-to-all-start.1 = ((bf16[32,2,2048]{2,1,0:T(2,128)(2,1)}), bf16[32,2,2048]{2,1,0:T(2,128)(2,1)S(1)}, u32[]{:S(2)}, u32[]{:S(2)}) async-start(bf16[32,2,2048]{2,1,0:T(2,128)(2,1)} %reshape.868), calls=%async_computation.1 | async-start | bytes 524288 | tf_op jit(solution)/shard_map/all_to_all | solution.py:105
  172.1 0.7 copy-start.7
  172.9 216.2 %all-to-all-start.4 = ((bf16[32,8,2,2,4096]{4,1,3,2,0:T(8,128)(2,1)}), bf16[32,8,2,2,4096]{4,1,3,2,0:T(8,128)(2,1)}, u32[]{:S(2)}, u32[]{:S(2)}) async-start(bf16[32,8,2,2,4096]{4,1,3,2,0:T(8,128)(2,1)} %copy.59), calls=%async_computation.4 | async-start | bytes 16777216 | tf_op jit(solution)/shard_map/all_to_all | solution.py:174
  182.8 268.1 %all-reduce.4.cloned.1.call-start = ((), (), s32[]{:S(2)}) async-start(), calls=%async_computation.9 | async-start | bytes 1048576 | tf_op jit(solution)/shard_map/psum | solution.py:21
  189.9 408.1 %reduce-scatter.2.cloned.1.call-start = ((), (), s32[]{:S(2)}) async-start(), calls=%async_computation.8 | async-start | bytes 9437184 | tf_op jit(solution)/shard_map/reduce_scatter | solution.py:176
  389.0 6.7 %copy-start.22 = (bf16[2,176,4096]{2,1,0:T(8,128)(2,1)S(1)}, bf16[2,176,4096]{2,1,0:T(8,128)(2,1)}, u32[]{:S(2)}) copy-start(bf16[2,176,4096]{2,1,0:T(8,128)(2,1)} %param.18) | copy-start | bytes 8650756
  418.7 0.9 copy-start.9
  421.0 20.7 %all-to-all-start = ((bf16[32,2,2048]{2,1,0:T(2,128)(2,1)}), bf16[32,2,2048]{2,1,0:T(2,128)(2,1)S(1)}, u32[]{:S(2)}, u32[]{:S(2)}) async-start(bf16[32,2,2048]{2,1,0:T(2,128)(2,1)} %reshape.870), calls=%async_computation | async-start | bytes 524288 | tf_op jit(solution)/shard_map/all_to_all | solution.py:104
  442.1 1.1 copy-start.2
  443.2 3.9 copy-start.10
  450.9 6.7 %copy-start.6 = (f32[512,1024]{1,0:T(8,128)S(1)}, f32[512,1024]{1,0:T(8,128)}, u32[]{:S(2)}) copy-start(f32[512,1024]{1,0:T(8,128)} %get-tuple-element.60) | copy-start | bytes 6291460
  457.1 1.0 copy-start.11
  458.1 1.6 copy-start.5
  460.2 1.6 copy-start.4
  462.3 1.6 copy-start.3
  463.9 1.1 copy-start.19
  463.9 1.1 copy-start.18
  463.9 1.1 copy-start.17
  463.9 1.2 copy-start.16
  463.9 1.2 copy-start.15
  463.9 1.2 copy-start.14
  463.9 1.2 copy-start.13
  463.9 1.2 copy-start.12
  472.9 128.2 %all-to-all-start.3 = ((bf16[32,2,2048]{2,1,0:T(2,128)(2,1)}), bf16[32,2,2048]{2,1,0:T(2,128)(2,1)S(1)}, u32[]{:S(2)}, u32[]{:S(2)}) async-start(bf16[32,2,2048]{2,1,0:T(2,128)(2,1)} %reshape.874), calls=%async_computation.3 | async-start | bytes 524288 | tf_op jit(solution)/shard_map/all_to_all | solution.py:158
  598.0 13.0 %copy-start.21 = (f32[64,2]{0,1:T(2,128)S(1)}, f32[64,2]{0,1:T(2,128)}, u32[]{:S(2)}) copy-start(f32[64,2]{0,1:T(2,128)} %param.16) | copy-start | bytes 1540
  601.0 34.1 %all-to-all-start.5 = ((bf16[32,4,4096]{2,1,0:T(4,128)(2,1)}), bf16[32,4,4096]{2,1,0:T(4,128)(2,1)S(1)}, u32[]{:S(2)}, u32[]{:S(2)}) async-start(bf16[32,4,4096]{2,1,0:T(4,128)(2,1)} %copy.63), calls=%async_computation.6 | async-start | bytes 2097152 | tf_op jit(solution)/shard_map/all_to_all | solution.py:180
  637.6 9.1 %copy-start.1 = (bf16[2,176,4096]{2,1,0:T(8,128)(2,1)S(1)}, bf16[2,176,4096]{2,1,0:T(8,128)(2,1)}, u32[]{:S(2)}) copy-start(bf16[2,176,4096]{2,1,0:T(8,128)(2,1)} %param.19) | copy-start | bytes 8650756
Sparse Core Ops, SparseCore 0:
  10.8 108.0 all-gather.2
  190.0 130.0 all-reduce.3
  418.8 179.1 reduce-scatter.1
where the time goes:
time: 666 us; the launch traced here: 653 us
  waiting for transfers between devices  403 us (61%)
  local copies, waits for them, and re-layouts  109 us (16%)
  starting transfers between devices  54.1 us (8%)
  matrix products  33.9 us (5%)
  blocking collectives  20.9 us (3%)
  other arithmetic  18.7 us (3%)
  between operations  14.7 us (2%)
    all_to_all x1, waiting for transfers between devices, on_device(): lax.all_to_all(send_rows, 'exp', split_axis=0, concat_axis=0, tiled=True)  199 us
    reduce_scatter x1, waiting for transfers between devices, on_device(): lax.psum_scatter(slice_term.astype(jnp.bfloat16), 'seq', scatter_dimensio...  120 us
    all_gather x1, waiting for transfers between devices, on_device(): lax.all_gather(normed, 'seq', axis=0, tiled=True)  45.5 us
    reshape x2, local copies, waits for them, and re-layouts, on_device(): send_rows.reshape(exp_count, seq_count, exp_dev, CAP, feature_count)  30.6 us
    all_to_all x1, waiting for transfers between devices, on_device(): lax.all_to_all(owner_out, 'exp', split_axis=0, concat_axis=0, tiled=True)  22.6 us
    all_gather x1, blocking collectives, on_device(): lax.all_gather(expert_ids, 'seq', axis=0, tiled=True)  20.9 us
    unnamed x72, local copies, waits for them, and re-layouts  19.5 us
    gather x1, local copies, waits for them, and re-layouts, fill_slots(): return padded[index_table]  17.8 us
  transfers between devices with their start and end apart: 9, of which 5 were waited for; matrix products, arithmetic and copies ran while one was open for 21% of the time, Pallas kernels for 0%

commit v1 on v0

v1 whole, which is shorter than its diff:
```python
import functools

import jax
import jax.numpy as jnp
from jax import lax
from jax.experimental import pallas as pl
from jax.experimental.pallas import tpu as pltpu
from jax.sharding import PartitionSpec as P

MESH = pl.DeviceIdType.MESH
BF = jnp.bfloat16
F32 = jnp.float32
EPS = 1e-05
NEG = -1e30

D = 4096
W = 1024
FFD = 176
FFP = 256
NT = (((1,), (1,)), ((), ()))

GATHER = (
    (0, 0, 64, 64, "p"),
    (0, 0, 256, 64, "+"),
    (0, 64, 320, 64, "+"),
    (0, 0, 128, 64, "-"),
    (0, 64, 192, 64, "-"),
    (0, 256, 384, 64, "+"),
    (0, 192, 448, 64, "-"),
    (1, 0, 256, 64, "+"),
    (1, 0, 128, 64, "-"),
    (1, 256, 384, 32, "+"),
    (1, 160, 416, 32, "-"),
    (1, 0, 64, 64, "p"),
    (1, 256, 320, 64, "p"),
    (1, 128, 192, 64, "p"),
    (1, 384, 448, 32, "p"),
    (1, 416, 480, 32, "p"),
)
REDUCE = (
    (0, 384, 64, "+"),
    (0, 448, 64, "-"),
    (0, 192, 64, "+"),
    (0, 128, 64, "+"),
    (0, 256, 64, "-"),
    (0, 320, 64, "-"),
    (0, 64, 64, "p"),
    (1, 448, 64, "p"),
    (1, 192, 64, "p"),
    (1, 320, 64, "p"),
    (1, 64, 64, "p"),
    (1, 384, 32, "+"),
    (1, 416, 32, "-"),
    (1, 128, 64, "+"),
    (1, 256, 64, "-"),
)


def iota(shape, dim):
    return lax.broadcasted_iota(jnp.int32, shape, dim)


def dot(a, b):
    return jnp.dot(a, b, preferred_element_type=F32)


def remote(src, dst, send, recv, device):
    return pltpu.make_async_remote_copy(
        src_ref=src,
        dst_ref=dst,
        send_sem=send,
        recv_sem=recv,
        device_id=device,
        device_id_type=MESH,
    )


def kernel(
    tok, gain, q, k, v, ids_t, ids, rw, gp, up, dp,
    att_out, mix_out,
    n4, sb, ab, xg, pb, wg, wu, wd, rb, f4, fb, cb,
    qb, kb, vb, smk, smv, ob, ao,
    w_sem, d_send, d_recv, c_send, c_recv, g_send, g_recv, r_send, r_recv,
    a_send, a_recv, s_send, s_recv, o_send, o_recv,
):
    me_s = lax.axis_index("seq")
    me_p = lax.axis_index("exp")
    me_y = lax.div(me_s, 2)
    me_z = lax.rem(me_s, 2)
    core = lax.rem(me_p, 2)
    chip = lax.div(me_p, 2)
    half = lax.div(me_p, 16)
    slot = lax.rem(me_p, 16)
    seg = 2 * me_s + core
    peer = {
        "+": (2 * lax.rem(me_y + 1, 4) + me_z, me_p),
        "-": (2 * lax.rem(me_y + 3, 4) + me_z, me_p),
        "p": (2 * me_y + 1 - me_z, me_p),
    }

    weights = [
        pltpu.make_async_copy(src, dst.at[:, pl.ds(0, FFD), :], w_sem.at[i])
        for i, (src, dst) in enumerate(((gp, wg), (up, wu), (dp, wd)))
    ]
    for copy in weights:
        copy.start()

    barrier = pltpu.get_barrier_semaphore()

    def greet_exp(j, carry):
        pl.semaphore_signal(
            barrier, inc=1, device_id=(me_s, lax.rem(me_p + j, 32)), device_id_type=MESH
        )
        return carry

    def greet_seq(j, carry):
        other = lax.rem(me_s + j, 8)
        pl.semaphore_signal(barrier, inc=1, device_id=(other, me_p), device_id_type=MESH)
        pl.semaphore_signal(
            barrier, inc=1, device_id=(other, me_p + 1 - 2 * core), device_id_type=MESH
        )
        return carry

    lax.fori_loop(1, 32, greet_exp, 0)
    lax.fori_loop(1, 8, greet_seq, 0)

    def norm_rows(i, carry):
        rows = pl.ds(pl.multiple_of(i * 16, 16), 16)
        vals = tok[rows, :].astype(F32)
        inv = lax.rsqrt(jnp.mean(vals * vals, axis=-1, keepdims=True) + EPS)
        normed = (vals * inv * gain[...]).astype(BF)
        for c in range(4):
            n4[pl.ds(pl.multiple_of(c * 64 + i * 16, 16), 16), :] = normed[:, c * W : c * W + W]
        return carry

    lax.fori_loop(0, 4, norm_rows, 0)

    row_j = iota((512, 64), 0)
    expert_j = 2 * (row_j // 16) + (row_j // 2) % 2
    named = ((ids_t[0:1, :] == expert_j) | (ids_t[1:2, :] == expert_j)).astype(F32)
    above = (iota((64, 64), 0) < iota((64, 64), 1)).astype(BF)
    before = dot(named.astype(BF), above)
    pick = jnp.where(before == (row_j % 2).astype(F32), named, 0.0)
    block_j = (row_j // 4) % 4
    pick4 = jnp.concatenate([jnp.where(block_j == c, pick, 0.0).astype(BF) for c in range(4)], axis=1)
    for n in range(2):
        cols = pl.ds(n * 512, 512)
        sb[:, cols] = dot(pick4, n4[:, cols]).astype(BF)

    pl.semaphore_wait(barrier, 45)

    def block_of(index):
        return pl.ds(pl.multiple_of(index * 16, 16), 16)

    def exchange(src, dst, send, recv):
        def start(j, carry):
            to = lax.rem(me_p + j, 32)
            remote(
                src.at[block_of(to), :], dst.at[block_of(me_p), :],
                send.at[to], recv.at[me_p], (me_s, to),
            ).start()
            return carry

        lax.fori_loop(1, 32, start, 0)

    def exchange_wait(src, dst, send, recv, sent):
        def wait(j, carry):
            other = lax.rem(me_p + j, 32)
            copy = remote(
                src.at[block_of(other), :], dst.at[block_of(other), :],
                send.at[other], recv.at[other], (me_s, other),
            )
            if sent:
                copy.wait_send()
            else:
                copy.wait_recv()
            return carry

        lax.fori_loop(1, 32, wait, 0)

    exchange(sb, ab, d_send, d_recv)

    def cols_of(index):
        return pl.ds(pl.multiple_of(index * 128, 128), 128)

    def toks_of(index):
        return pl.ds(pl.multiple_of(index * 64, 64), 64)

    def heads_start(j, carry):
        m = lax.rem(chip + j, 16)
        to = 2 * m + half
        for i, (src, dst) in enumerate(((k, kb), (v, vb), (q, qb))):
            piece, land = src.at[:, cols_of(m)], dst.at[toks_of(slot), :]

            @pl.when(to != me_p)
            def _():
                remote(piece, land, a_send.at[i, m], a_recv.at[i, slot], (me_s, to)).start()

            @pl.when(to == me_p)
            def _():
                pltpu.make_async_copy(piece, land, a_recv.at[i, slot]).start()

        return carry

    lax.fori_loop(0, 16, heads_start, 0)

    def heads_wait(j, carry):
        for i, dst in enumerate((kb, vb, qb)):
            land = dst.at[toks_of(j), :]
            pltpu.make_async_copy(land, land, a_recv.at[i, j]).wait()
        return carry

    def heads_sent(j, carry):
        for i, (src, dst) in enumerate(((k, kb), (v, vb), (q, qb))):

            @pl.when(2 * j + half != me_p)
            def _():
                remote(
                    src.at[:, cols_of(j)], dst.at[toks_of(slot), :],
                    a_send.at[i, j], a_recv.at[i, slot], (me_s, 2 * j + half),
                ).wait_send()

        return carry

    def zero_rows(i, carry):
        rows = pl.ds(pl.multiple_of(FFD + i * 16, 16), 16)
        for e in range(2):
            for ref in (wg, wu, wd):
                ref[e, rows, :] = jnp.zeros((16, D), BF)
        return carry

    lax.fori_loop(0, 5, zero_rows, 0)

    ab[block_of(me_p), :] = sb[block_of(me_p), :]
    exchange_wait(sb, ab, d_send, d_recv, False)
    out_i, in_i = iota((128, 512), 0), iota((128, 512), 1)
    home = ((out_i % 64) // 2) * 16 + (out_i // 64) * 2 + out_i % 2

    for c in range(4):
        order = (in_i == home + 4 * c).astype(BF)
        rows = dot(order, ab[...]).astype(BF)
        xg[0, 0:64, c * W : c * W + W] = rows[0:64]
        xg[1, 0:64, c * W : c * W + W] = rows[64:128]

    def gather(i):
        e, src, dst, n, way = GATHER[i]
        return remote(
            xg.at[e, pl.ds(src, n), :], xg.at[e, pl.ds(dst, n), :],
            g_send.at[i], g_recv.at[i], peer[way],
        )

    def arrived(i):
        e, _, dst, n, way = GATHER[i]
        ref = xg.at[e, pl.ds(dst, n), :]
        remote(ref, ref, g_send.at[i], g_recv.at[i], peer[way]).wait_recv()

    for i in (0, 7, 8, 1, 3, 11):
        gather(i).start()

    lax.fori_loop(0, 16, heads_wait, 0)
    blocks = (iota((64, 1024), 1) // 16 == iota((64, 1024), 0)).astype(BF)
    mine = toks_of(seg)
    smk[mine, :] = (dot(blocks, kb[...]) * 0.25).astype(BF)
    smv[mine, :] = (dot(blocks, vb[...]) * 0.25).astype(BF)

    def sums(g, src_seg):
        other = (lax.div(g, 2), 2 * chip + lax.rem(g, 2))
        for i, ref in enumerate((smk, smv)):
            yield remote(
                ref.at[toks_of(src_seg), :], ref.at[toks_of(src_seg), :],
                s_send.at[i, g], s_recv.at[i, src_seg], other,
            )

    def sums_start(g, carry):
        for copy in sums(g, seg):
            copy.start()
        return carry

    def sums_sent(g, carry):
        for copy in sums(g, seg):
            copy.wait_send()
        return carry

    def sums_wait(g, carry):
        for copy in sums(g, g):
            copy.wait_recv()
        return carry

    def sums_zero(g, carry):
        smk[toks_of(g), :] = jnp.zeros((64, 128), BF)
        smv[toks_of(g), :] = jnp.zeros((64, 128), BF)
        return carry

    lax.fori_loop(seg + 1, 16, sums_start, 0)
    lax.fori_loop(seg + 1, 16, sums_zero, 0)

    arrived(0)
    gather(2).start()
    gather(4).start()
    arrived(7)
    gather(9).start()
    gather(12).start()
    arrived(8)
    gather(10).start()
    gather(13).start()

    lax.fori_loop(0, seg, sums_wait, 0)

    def attend(step, carry):
        rows = pl.ds(pl.multiple_of(lax.div(step, 2) * 128, 128), 128)
        head = lax.rem(step, 2)
        lane = iota((128, 128), 1) // 64 == head
        query = jnp.where(lane, qb[rows, :].astype(F32) * 0.125, 0.0).astype(BF)
        local = lax.dot_general(query, kb[...], NT, preferred_element_type=F32)
        summ = lax.dot_general(query, smk[...], NT, preferred_element_type=F32)
        pos = lax.div(step, 2) * 128 + iota((128, 1024), 0)
        col = iota((128, 1024), 1)
        local = jnp.where(col <= pos, local, NEG)
        summ = jnp.where(col < seg * 64, summ, NEG)
        top = jnp.maximum(
            jnp.max(local, axis=-1, keepdims=True), jnp.max(summ, axis=-1, keepdims=True)
        )
        local = jnp.exp(local - top)
        summ = jnp.exp(summ - top)
        total = jnp.sum(local, axis=-1, keepdims=True) + jnp.sum(summ, axis=-1, keepdims=True)
        mixed = (dot(local.astype(BF), vb[...]) + dot(summ.astype(BF), smv[...])) / total
        ob[rows, :] = jnp.where(lane, mixed, ob[rows, :].astype(F32)).astype(BF)
        return carry

    ob[...] = jnp.zeros((1024, 128), BF)
    lax.fori_loop(0, 8, attend, 0)
    arrived(1)
    gather(5).start()
    arrived(4)
    gather(6).start()
    arrived(9)
    gather(14).start()
    arrived(10)
    gather(15).start()
    lax.fori_loop(8, 16, attend, 0)

    def back_start(j, carry):
        i = lax.rem(slot + j, 16)
        to = 16 * core + i
        piece, land = ob.at[toks_of(i), :], ao.at[:, cols_of(chip)]

        @pl.when(to != me_p)
        def _():
            remote(piece, land, o_send.at[i], o_recv.at[chip], (me_s, to)).start()

        @pl.when(to == me_p)
        def _():
            pltpu.make_async_copy(piece, land, o_recv.at[chip]).start()

        return carry

    def back_wait(m, carry):
        land = ao.at[:, cols_of(m)]
        pltpu.make_async_copy(land, land, o_recv.at[m]).wait()
        return carry

    def back_sent(i, carry):
        @pl.when(16 * core + i != me_p)
        def _():
            remote(
                ob.at[toks_of(i), :], ao.at[:, cols_of(chip)],
                o_send.at[i], o_recv.at[chip], (me_s, 16 * core + i),
            ).wait_send()

        return carry

    lax.fori_loop(0, 16, back_start, 0)

    def expert(e, group):
        rows = pl.ds(pl.multiple_of(group * 128, 128), 128)
        gate = jnp.zeros((128, FFP), F32)
        high = jnp.zeros((128, FFP), F32)
        for c in range(4):
            part = xg[e, rows, c * W : c * W + W]
            gate += lax.dot_general(
                part, wg[e, :, c * W : c * W + W], NT, preferred_element_type=F32
            )
            high += lax.dot_general(
                part, wu[e, :, c * W : c * W + W], NT, preferred_element_type=F32
            )
        hidden = (gate / (1.0 + jnp.exp(-gate)) * high).astype(BF)
        for c in range(8):
            pb[e, rows, c * 512 : c * 512 + 512] = dot(
                hidden, wd[e, :, c * 512 : c * 512 + 512]
            ).astype(BF)

    def experts(first, groups):
        def step(i, carry):
            expert(lax.rem(i, 2), first + lax.div(i, 2))
            return carry

        lax.fori_loop(0, 2 * groups, step, 0)

    def reduce(i):
        e, src, n, way = REDUCE[i]
        return remote(
            pb.at[e, pl.ds(src, n), :], rb.at[i, pl.ds(0, n), :],
            r_send.at[i], r_recv.at[i], peer[way],
        )

    def landed(i):
        _, _, n, way = REDUCE[i]
        ref = rb.at[i, pl.ds(0, n), :]
        remote(ref, ref, r_send.at[i], r_recv.at[i], peer[way]).wait_recv()

    def add_into(e, first, n, *terms):
        def step(i, carry):
            rows = pl.ds(pl.multiple_of(first + i * 16, 16), 16)
            total = pb[e, rows, :].astype(F32)
            for term in terms:
                total += rb[term, pl.ds(pl.multiple_of(i * 16, 16), 16), :].astype(F32)
            pb[e, rows, :] = total.astype(BF)
            return carry

        lax.fori_loop(0, n // 16, step, 0)

    def finish(e, *terms):
        def step(i, carry):
            rows = pl.ds(pl.multiple_of(i * 16, 16), 16)
            total = pb[e, rows, :].astype(F32)
            for term in terms:
                total += rb[term, rows, :].astype(F32)
            total = total.astype(BF)
            for c in range(4):
                place = pl.ds(pl.multiple_of(c * 128 + e * 64 + i * 16, 16), 16)
                f4[place, :] = total[:, c * W : c * W + W]
            return carry

        lax.fori_loop(0, 4, step, 0)

    for copy in weights:
        copy.wait()
    arrived(11)
    experts(0, 1)
    reduce(10).start()
    arrived(2)
    arrived(3)
    arrived(12)
    arrived(13)
    experts(1, 2)
    for i in (2, 4, 8, 9):
        reduce(i).start()
    arrived(5)
    arrived(6)
    arrived(14)
    arrived(15)
    experts(3, 1)
    for i in (0, 1, 7):
        reduce(i).start()

    landed(8)
    add_into(1, 128, 64, 8)
    landed(9)
    add_into(1, 256, 64, 9)
    landed(7)
    add_into(1, 384, 64, 7)
    reduce(11).start()
    reduce(12).start()
    landed(0)
    add_into(0, 128, 64, 0)
    reduce(3).start()
    landed(1)
    add_into(0, 320, 64, 1)
    reduce(5).start()
    landed(11)
    add_into(1, 128, 32, 11)
    reduce(13).start()
    landed(12)

    def add_upper(i, carry):
        rows = pl.ds(pl.multiple_of(288 + i * 16, 16), 16)
        part = rb[12, pl.ds(pl.multiple_of(i * 16, 16), 16), :].astype(F32)
        pb[1, rows, :] = (pb[1, rows, :].astype(F32) + part).astype(BF)
        return carry

    lax.fori_loop(0, 2, add_upper, 0)
    reduce(14).start()
    landed(2)
    landed(5)
    add_into(0, 64, 64, 2, 5)
    reduce(6).start()
    landed(10)
    landed(13)
    landed(14)
    finish(1, 10, 13, 14)
    landed(3)
    landed(4)
    landed(6)
    finish(0, 3, 4, 6)

    out_o, in_o = iota((512, 512), 0), iota((512, 512), 1)
    place = ((out_o // 4) % 4) * 128 + ((out_o // 2) % 2) * 64 + (out_o // 16) * 2 + out_o % 2
    order = (in_o == place).astype(BF)
    for n in range(2):
        cols = pl.ds(n * 512, 512)
        fb[:, cols] = dot(order, f4[:, cols]).astype(BF)
    exchange(fb, cb, c_send, c_recv)
    cb[block_of(me_p), :] = fb[block_of(me_p), :]

    col_j = iota((64, 512), 1)
    expert_c = 2 * (col_j // 16) + (col_j // 2) % 2
    first = ids[:, 0:1] == expert_c
    second = ids[:, 1:2] == expert_c
    named_c = (first | second).astype(BF)
    below = (iota((64, 64), 1) < iota((64, 64), 0)).astype(BF)
    before_c = dot(below, named_c)
    share = jnp.where(first, rw[:, 0:1], 0.0) + jnp.where(second, rw[:, 1:2], 0.0)
    share = jnp.where(before_c == (col_j % 2).astype(F32), share, 0.0)
    big = share.astype(BF)
    small = (share - big.astype(F32)).astype(BF)
    block_c = (col_j // 4) % 4

    lax.fori_loop(0, 16, back_wait, 0)
    att_out[...] = ao[...]

    exchange_wait(fb, cb, c_send, c_recv, False)
    none = jnp.zeros((64, 512), BF)
    for c in range(4):
        mix = dot(jnp.where(block_c == c, big, none), cb[...])
        mix += dot(jnp.where(block_c == c, small, none), cb[...])
        mix_out[:, c * W : c * W + W] = mix.astype(BF)

    exchange_wait(sb, ab, d_send, d_recv, True)
    exchange_wait(fb, cb, c_send, c_recv, True)
    lax.fori_loop(0, 16, heads_sent, 0)
    lax.fori_loop(0, 16, back_sent, 0)
    lax.fori_loop(seg + 1, 16, sums_sent, 0)
    for i in range(len(GATHER)):
        gather(i).wait_send()
    for i in range(len(REDUCE)):
        reduce(i).wait_send()


def on_device(tokens, gain, queries, keys, values, ids, rw, gate, up, down):
    vmem = pl.BlockSpec(memory_space=pltpu.VMEM)
    hbm = pl.BlockSpec(memory_space=pl.ANY)
    dma = pltpu.SemaphoreType.DMA
    return pl.pallas_call(
        kernel,
        out_shape=(
            jax.ShapeDtypeStruct((64, 2048), BF),
            jax.ShapeDtypeStruct((64, D), BF),
        ),
        in_specs=[vmem, vmem, hbm, hbm, hbm, vmem, vmem, vmem, hbm, hbm, hbm],
        out_specs=(vmem, vmem),
        scratch_shapes=[
            pltpu.VMEM((256, W), BF),
            pltpu.VMEM((512, W), BF),
            pltpu.VMEM((512, W), BF),
            pltpu.VMEM((2, 512, D), BF),
            pltpu.VMEM((2, 512, D), BF),
            pltpu.VMEM((2, FFP, D), BF),
            pltpu.VMEM((2, FFP, D), BF),
            pltpu.VMEM((2, FFP, D), BF),
            pltpu.VMEM((15, 64, D), BF),
            pltpu.VMEM((512, W), BF),
            pltpu.VMEM((512, W), BF),
            pltpu.VMEM((512, W), BF),
            pltpu.VMEM((1024, 128), BF),
            pltpu.VMEM((1024, 128), BF),
            pltpu.VMEM((1024, 128), BF),
            pltpu.VMEM((1024, 128), BF),
            pltpu.VMEM((1024, 128), BF),
            pltpu.VMEM((1024, 128), BF),
            pltpu.VMEM((64, 2048), BF),
            dma((3,)),
            dma((32,)),
            dma((32,)),
            dma((32,)),
            dma((32,)),
            dma((len(GATHER),)),
            dma((len(GATHER),)),
            dma((len(REDUCE),)),
            dma((len(REDUCE),)),
            dma((3, 16)),
            dma((3, 16)),
            dma((2, 16)),
            dma((2, 16)),
            dma((16,)),
            dma((16,)),
        ],
        compiler_params=pltpu.CompilerParams(
            collective_id=0, has_side_effects=True, vmem_limit_bytes=60 * 1024 * 1024
        ),
        name="layer",
    )(tokens, gain.reshape(1, D), queries, keys, values, ids.T, ids, rw, gate, up, down)


def solution(mesh):
    rows = P(("seq", "exp"), None)
    parts = P("exp", "seq", None)
    return jax.shard_map(
        on_device,
        mesh=mesh,
        in_specs=(rows, P(), rows, rows, rows, rows, rows, parts, parts, parts),
        out_specs=(rows, rows),
        check_vma=False,
    )
```

time: 666 us -> 234 us (0.35); the launches traced: 653 us -> 234 us
  waiting for transfers between devices: 403 us -> 0 us
  Pallas kernels: 0 us -> 227 us
  local copies, waits for them, and re-layouts: 109 us -> 6.3 us
  starting transfers between devices: 54.1 us -> 0 us
  matrix products: 33.9 us -> 0 us
  blocking collectives: 20.9 us -> 0 us
  other arithmetic: 18.7 us -> 0 us
  between operations: 14.7 us -> 0.64 us
    all_to_all x6 -> x0, waiting for transfers between devices: 237 us -> none  [the longest x1 199 us: on_device(): lax.all_to_all(send_rows, 'exp', split_axis=0, concat_axis=0, tiled=True)]
    pallas_call x0 -> x1, Pallas kernels: none -> 227 us  [on_device(): pl.pallas_call(kernel, out_shape=(jax.ShapeDtypeStruct((64, 2048), BF), j...]
    reduce_scatter x1 -> x0, waiting for transfers between devices: 120 us -> none  [on_device(): lax.psum_scatter(slice_term.astype(jnp.bfloat16), 'seq', scatter_dimensio...]
    all_to_all x6 -> x0, starting transfers between devices: 53.6 us -> none  [the longest x1 12.6 us: on_device(): lax.all_to_all(attn_values, 'exp', split_axis=1, concat_axis=0, tiled=True)]
    all_gather x1 -> x0, waiting for transfers between devices: 45.5 us -> none  [on_device(): lax.all_gather(normed, 'seq', axis=0, tiled=True)]
    reshape x6 -> x0, local copies, waits for them, and re-layouts: 35.3 us -> none  [the longest x2 30.6 us: on_device(): send_rows.reshape(exp_count, seq_count, exp_dev, CAP, feature_count)]
    dot_general x19 -> x0, matrix products: 33.9 us -> none  [the longest x4 7.5 us: attend_block(): jnp.einsum('qhd,khd->hqk', query_blk, seg_keys, preferred_element_type=jn...]
    all_gather x1 -> x0, blocking collectives: 20.9 us -> none  [on_device(): lax.all_gather(expert_ids, 'seq', axis=0, tiled=True)]
  transfers between devices with their start and end apart: 9 -> 0, of which waited for: 5 -> 0; matrix products, arithmetic and copies ran while one was open for 21% -> 0% of each run, Pallas kernels for 0% -> 0%
where the time goes in v1:
time: 234 us
  Pallas kernels  227 us (97%)
  local copies, waits for them, and re-layouts  6.3 us (3%)
    pallas_call x1, Pallas kernels, on_device(): pl.pallas_call(kernel, out_shape=(jax.ShapeDtypeStruct((64, 2048), BF), j...  227 us
    unnamed x4, local copies, waits for them, and re-layouts  6.3 us

profile of v1, /device:TPU:1, one launch (start us, length us, event | category | flops | bytes accessed | tf_op | source)
XLA Modules:
  0.0 234.1 jit_solution(7506666720046986757)
XLA Ops:
  0.6 1.4 copy.13.rw
  2.0 1.4 copy.12.ids
  3.4 227.1 %layer.1 = (bf16[64,2048]{1,0:T(8,128)(2,1)}, bf16[64,4096]{1,0:T(8,128)(2,1)}) custom-call(bf16[64,4096]{1,0:T(8,128)(2,1)} %tok.1, f32[1,4096]{1,0:T(1,128)} %bitcast.2, bf16[64,2048]{1,0:T(8,128)(2,1)} %q.1, bf16[64,2048]{1,0:T(8,128)(2,1)} %k.1, bf16[64,2048]{1,0:T(8,128)(2,1)} %v.1, s32[2,64]{1,0:T(2,128)} %bitcast.3, s32[64,2]{1,0:T(8,128)} %copy.12.ids, ...), custom_call_target="tpu_custom_call" | custom-call | tf_op jit(solution)/shard_map/layer/pallas_call | solution.py:543
  230.5 1.7 copy.16
  232.2 1.9 copy.17

commit v2 on v1

v2 whole, which is shorter than its diff:
```python
import functools

import jax
import jax.numpy as jnp
from jax import lax
from jax.experimental import pallas as pl
from jax.experimental.pallas import tpu as pltpu
from jax.sharding import PartitionSpec as P

MESH = pl.DeviceIdType.MESH
BF = jnp.bfloat16
F32 = jnp.float32
EPS = 1e-05
NEG = -1e30

D = 4096
W = 256
FFD = 176
FFP = 256
NT = (((1,), (1,)), ((), ()))

STREAMS = ((0, 0, 32, True), (0, 32, 32, True), (1, 0, 32, True), (1, 32, 32, False))


def plan():
    gather, reduce = {}, {}
    for t, (e, off, n, z_first) in enumerate(STREAMS):
        h = n // 2

        def at(group, z, off=off):
            return group * 128 + z * 64 + off

        g = {
            "p": (at(0, 0), at(0, 1), n, "p"),
            "+o": (at(0, 0), at(2, 0), n, "+"),
            "-o": (at(0, 0), at(1, 0), n, "-"),
        }
        if z_first:
            g["+x"] = (at(0, 1), at(2, 1), n, "+")
            g["-x"] = (at(0, 1), at(1, 1), n, "-")
            g["+f"] = (at(2, 0), at(3, 0), n, "+")
            g["-f"] = (at(1, 1), at(3, 1), n, "-")
            r = {
                "+2": (at(3, 0), n, "+"),
                "-2": (at(3, 1), n, "-"),
                "+x": (at(1, 1), n, "+"),
                "+s": (at(1, 0), n, "+"),
                "-x": (at(2, 0), n, "-"),
                "-s": (at(2, 1), n, "-"),
                "p": (at(0, 1), n, "p"),
            }
        else:
            g["+f"] = (at(2, 0), at(3, 0), h, "+")
            g["-f"] = (at(1, 0) + h, at(3, 0) + h, h, "-")
            g["p-"] = (at(2, 0), at(2, 1), n, "p")
            g["p+"] = (at(1, 0), at(1, 1), n, "p")
            g["pl"] = (at(3, 0), at(3, 1), h, "p")
            g["pu"] = (at(3, 0) + h, at(3, 1) + h, h, "p")
            r = {
                "p2": (at(3, 1), n, "p"),
                "p+": (at(1, 1), n, "p"),
                "p-": (at(2, 1), n, "p"),
                "p": (at(0, 1), n, "p"),
                "+2": (at(3, 0), h, "+"),
                "-2": (at(3, 0) + h, h, "-"),
                "+s": (at(1, 0), n, "+"),
                "-s": (at(2, 0), n, "-"),
            }
        for name, entry in g.items():
            gather[t, name] = (len(gather), e, *entry)
        for name, entry in r.items():
            reduce[t, name] = (len(reduce), e, *entry)
    rows = {}
    total = 0
    for key, (_, _, _, n, _) in reduce.items():
        rows[key] = total
        total += n
    return gather, reduce, rows, total


GATHER, REDUCE, LANDING, LANDING_ROWS = plan()


def iota(shape, dim):
    return lax.broadcasted_iota(jnp.int32, shape, dim)


def dot(a, b):
    return jnp.dot(a, b, preferred_element_type=F32)


def remote(src, dst, send, recv, device):
    return pltpu.make_async_remote_copy(
        src_ref=src,
        dst_ref=dst,
        send_sem=send,
        recv_sem=recv,
        device_id=device,
        device_id_type=MESH,
    )


def kernel(
    tok, gain, q, k, v, ids, rw, gp, up, dp,
    att_out, mix_out,
    normed, there, back, stack, sb, ab, xg, pb, wg, wu, wd, rb, fb, cb, rows_in, share,
    qb, kb, vb, smk, smv, ob, ao,
    w_sem, d_send, d_recv, c_send, c_recv, g_send, g_recv, r_send, r_recv,
    a_send, a_recv, s_send, s_recv, o_send, o_recv,
):
    me_s = lax.axis_index("seq")
    me_p = lax.axis_index("exp")
    me_y = lax.div(me_s, 2)
    me_z = lax.rem(me_s, 2)
    core = lax.rem(me_p, 2)
    chip = lax.div(me_p, 2)
    half = lax.div(me_p, 16)
    slot = lax.rem(me_p, 16)
    seg = 2 * me_s + core
    peer = {
        "+": (2 * lax.rem(me_y + 1, 4) + me_z, me_p),
        "-": (2 * lax.rem(me_y + 3, 4) + me_z, me_p),
        "p": (2 * me_y + 1 - me_z, me_p),
    }

    barrier = pltpu.get_barrier_semaphore()

    def greet_exp(j, carry):
        to = lax.rem(me_z * 32 + me_p + j, 64)
        pl.semaphore_signal(
            barrier, inc=1, device_id=(2 * me_y + lax.div(to, 32), lax.rem(to, 32)),
            device_id_type=MESH,
        )
        return carry

    def greet_seq(j, carry):
        other = lax.rem(2 * me_y + j, 8)
        pl.semaphore_signal(barrier, inc=1, device_id=(other, me_p), device_id_type=MESH)
        pl.semaphore_signal(
            barrier, inc=1, device_id=(other, me_p + 1 - 2 * core), device_id_type=MESH
        )
        return carry

    lax.fori_loop(1, 64, greet_exp, 0)
    lax.fori_loop(2, 8, greet_seq, 0)

    weights = [
        pltpu.make_async_copy(src, dst.at[:, pl.ds(0, FFD), :], w_sem.at[i])
        for i, (src, dst) in enumerate(((gp, wg), (up, wu), (dp, wd)))
    ]
    for copy in weights:
        copy.start()

    row_j = iota((128, 64), 0)
    expert_j = 2 * (row_j % 32) + row_j // 64
    first = ids[0:1, :] == expert_j
    second = ids[1:2, :] == expert_j
    named = (first | second).astype(F32)
    above = (iota((64, 64), 0) < iota((64, 64), 1)).astype(BF)
    before = dot(named.astype(BF), above)
    pick = jnp.where(before == ((row_j // 32) % 2).astype(F32), named, 0.0)

    def norm_rows(i, carry):
        rows = pl.ds(pl.multiple_of(i * 16, 16), 16)
        vals = tok[rows, :].astype(F32)
        inv = lax.rsqrt(jnp.mean(vals * vals, axis=-1, keepdims=True) + EPS)
        normed[rows, :] = (vals * inv * gain[...]).astype(BF)
        return carry

    lax.fori_loop(0, 4, norm_rows, 0)

    out_i, in_i = iota((512, 512), 0), iota((512, 512), 1)
    there[...] = (in_i == (out_i % 16) * 32 + out_i // 16).astype(BF)
    back[...] = (in_i == (out_i % 32) * 16 + out_i // 32).astype(BF)

    for c in range(8):
        cols = slice(c * 512, c * 512 + 512)
        picked = dot(pick.astype(BF), normed[:, cols]).astype(BF)
        for t in range(4):
            for d in range(2):
                place = slice((2 * c + d) * 32, (2 * c + d) * 32 + 32)
                stack[t, place, :] = picked[32 * t : 32 * t + 32, d * W : d * W + W]
    for t in range(4):
        sb[t] = dot(there[...], stack[t]).astype(BF)

    pl.semaphore_wait(barrier, 75)

    def block_of(index):
        return pl.ds(pl.multiple_of(index * 16, 16), 16)

    me_x = lax.div(me_p, 8)
    me_h = lax.rem(lax.div(me_p, 2), 4)
    own_place = 2 * me_x + core

    def owner_of(j):
        to = lax.rem(me_p + j, 32)
        delta = lax.rem(lax.rem(lax.div(to, 2), 4) + 4 - me_h, 4)
        low = jnp.where(delta == 1, 0, jnp.where(delta == 3, 1, 1 - me_z))
        low = jnp.where(delta == 0, me_z, low)
        group = jnp.where(delta == 2, 3, jnp.where(low == me_z, 1, 2))
        group = jnp.where(delta == 0, 0, group)
        return to, 2 * me_y + low, 8 * group + own_place

    def source_of(j):
        place = lax.rem(own_place + j, 32)
        group = lax.div(place, 8)
        delta = jnp.where(group == 0, 0, jnp.where(group == 3, 2, 1 + 2 * me_z))
        low = jnp.where(group < 2, me_z, 1 - me_z)
        high = lax.rem(me_h + 4 - delta, 4)
        column = lax.div(lax.rem(place, 8), 2) * 8 + high * 2 + lax.rem(place, 2)
        return place, 2 * me_y + low, column

    def go_out(t, start):
        def step(j, carry):
            to, row, place = owner_of(j)
            copy = remote(
                sb.at[t, block_of(to), :], ab.at[t, block_of(place), :],
                d_send.at[t, to], d_recv.at[t, place], (row, to),
            )
            if start:
                copy.start()
            else:
                copy.wait_send()
            return carry

        lax.fori_loop(1, 32, step, 0)

    def go_home(t, start):
        def step(j, carry):
            place, row, column = source_of(j)
            copy = remote(
                fb.at[t, block_of(place), :], cb.at[t, block_of(me_p), :],
                c_send.at[t, place], c_recv.at[t, me_p], (row, column),
            )
            if start:
                copy.start()
            else:
                copy.wait_send()
            return carry

        lax.fori_loop(1, 32, step, 0)

    def came(t, dst, recv, own):
        def step(j, carry):
            place = lax.rem(own + j, 32)
            ref = dst.at[t, block_of(place), :]
            remote(ref, ref, d_send.at[t, place], recv.at[t, place], peer["p"]).wait_recv()
            return carry

        lax.fori_loop(1, 32, step, 0)

    go_out(0, True)
    go_out(1, True)

    part = jnp.where(first, rw[0:1, :], 0.0) + jnp.where(second, rw[1:2, :], 0.0)
    part = part * pick
    big = part.astype(BF)
    small = (part - big.astype(F32)).astype(BF)
    eye = (iota((64, 64), 0) == iota((64, 64), 1)).astype(BF)
    share[0] = lax.dot_general(eye, big, NT, preferred_element_type=F32).astype(BF)
    share[1] = lax.dot_general(eye, small, NT, preferred_element_type=F32).astype(BF)
    for t in range(4):
        ab[t, block_of(own_place), :] = sb[t, block_of(me_p), :]

    def zero_rows(i, carry):
        rows = pl.ds(pl.multiple_of(FFD + i * 16, 16), 16)
        for e in range(2):
            for ref in (wg, wu, wd):
                ref[e, rows, :] = jnp.zeros((16, D), BF)
        return carry

    lax.fori_loop(0, 5, zero_rows, 0)

    def cols_of(index):
        return pl.ds(pl.multiple_of(index * 128, 128), 128)

    def toks_of(index):
        return pl.ds(pl.multiple_of(index * 64, 64), 64)

    def heads_start(j, carry):
        m = lax.rem(chip + j, 16)
        to = 2 * m + half
        for i, (src, dst) in enumerate(((k, kb), (v, vb), (q, qb))):
            piece, land = src.at[:, cols_of(m)], dst.at[toks_of(slot), :]

            @pl.when(to != me_p)
            def _():
                remote(piece, land, a_send.at[i, m], a_recv.at[i, slot], (me_s, to)).start()

            @pl.when(to == me_p)
            def _():
                pltpu.make_async_copy(piece, land, a_recv.at[i, slot]).start()

        return carry

    def heads_wait(j, carry):
        for i, dst in enumerate((kb, vb, qb)):
            land = dst.at[toks_of(j), :]
            pltpu.make_async_copy(land, land, a_recv.at[i, j]).wait()
        return carry

    def heads_sent(j, carry):
        for i, (src, dst) in enumerate(((k, kb), (v, vb), (q, qb))):

            @pl.when(2 * j + half != me_p)
            def _():
                remote(
                    src.at[:, cols_of(j)], dst.at[toks_of(slot), :],
                    a_send.at[i, j], a_recv.at[i, slot], (me_s, 2 * j + half),
                ).wait_send()

        return carry

    def sort_rows(t):
        came(t, ab, d_recv, own_place)
        e, off, n, _ = STREAMS[t]
        rows = dot(back[...], ab[t]).astype(BF)
        for c in range(16):
            xg[e, off : off + n, c * W : c * W + W] = rows[32 * c : 32 * c + 32]

    def gather(t, name):
        i, e, src, dst, n, way = GATHER[t, name]
        return remote(
            xg.at[e, pl.ds(src, n), :], xg.at[e, pl.ds(dst, n), :],
            g_send.at[i], g_recv.at[i], peer[way],
        )

    def spread(t, *names):
        for name in names:
            gather(t, name).start()

    def arrived(t, *names):
        for name in names:
            i, e, _, dst, n, way = GATHER[t, name]
            ref = xg.at[e, pl.ds(dst, n), :]
            remote(ref, ref, g_send.at[i], g_recv.at[i], peer[way]).wait_recv()

    def summarize():
        blocks = (iota((64, 1024), 1) // 16 == iota((64, 1024), 0)).astype(BF)
        mine = toks_of(seg)
        smk[mine, :] = (dot(blocks, kb[...]) * 0.25).astype(BF)
        smv[mine, :] = (dot(blocks, vb[...]) * 0.25).astype(BF)

    def sums(g, src_seg):
        other = (lax.div(g, 2), 2 * chip + lax.rem(g, 2))
        for i, ref in enumerate((smk, smv)):
            yield remote(
                ref.at[toks_of(src_seg), :], ref.at[toks_of(src_seg), :],
                s_send.at[i, g], s_recv.at[i, src_seg], other,
            )

    def sums_start(g, carry):
        for copy in sums(g, seg):
            copy.start()
        return carry

    def sums_sent(g, carry):
        for copy in sums(g, seg):
            copy.wait_send()
        return carry

    def sums_wait(g, carry):
        for copy in sums(g, g):
            copy.wait_recv()
        return carry

    def sums_zero(g, carry):
        smk[toks_of(g), :] = jnp.zeros((64, 128), BF)
        smv[toks_of(g), :] = jnp.zeros((64, 128), BF)
        return carry

    def attend(step, carry):
        rows = pl.ds(pl.multiple_of(lax.div(step, 2) * 128, 128), 128)
        head = lax.rem(step, 2)
        lane = iota((128, 128), 1) // 64 == head
        query = jnp.where(lane, qb[rows, :].astype(F32) * 0.125, 0.0).astype(BF)
        local = lax.dot_general(query, kb[...], NT, preferred_element_type=F32)
        summ = lax.dot_general(query, smk[...], NT, preferred_element_type=F32)
        pos = lax.div(step, 2) * 128 + iota((128, 1024), 0)
        col = iota((128, 1024), 1)
        local = jnp.where(col <= pos, local, NEG)
        summ = jnp.where(col < seg * 64, summ, NEG)
        top = jnp.maximum(
            jnp.max(local, axis=-1, keepdims=True), jnp.max(summ, axis=-1, keepdims=True)
        )
        local = jnp.exp(local - top)
        summ = jnp.exp(summ - top)
        total = jnp.sum(local, axis=-1, keepdims=True) + jnp.sum(summ, axis=-1, keepdims=True)
        mixed = (dot(local.astype(BF), vb[...]) + dot(summ.astype(BF), smv[...])) / total
        ob[rows, :] = jnp.where(lane, mixed, ob[rows, :].astype(F32)).astype(BF)
        return carry

    def back_start(j, carry):
        i = lax.rem(slot + j, 16)
        to = 16 * core + i
        piece, land = ob.at[toks_of(i), :], ao.at[:, cols_of(chip)]

        @pl.when(to != me_p)
        def _():
            remote(piece, land, o_send.at[i], o_recv.at[chip], (me_s, to)).start()

        @pl.when(to == me_p)
        def _():
            pltpu.make_async_copy(piece, land, o_recv.at[chip]).start()

        return carry

    def back_wait(m, carry):
        land = ao.at[:, cols_of(m)]
        pltpu.make_async_copy(land, land, o_recv.at[m]).wait()
        return carry

    def back_sent(i, carry):
        @pl.when(16 * core + i != me_p)
        def _():
            remote(
                ob.at[toks_of(i), :], ao.at[:, cols_of(chip)],
                o_send.at[i], o_recv.at[chip], (me_s, 16 * core + i),
            ).wait_send()

        return carry

    def expert(e, group):
        rows = pl.ds(pl.multiple_of(group * 128, 128), 128)
        gate = jnp.zeros((128, FFP), F32)
        high = jnp.zeros((128, FFP), F32)
        for c in range(4):
            cols = slice(c * 1024, c * 1024 + 1024)
            part = xg[e, rows, cols]
            gate += lax.dot_general(part, wg[e, :, cols], NT, preferred_element_type=F32)
            high += lax.dot_general(part, wu[e, :, cols], NT, preferred_element_type=F32)
        hidden = (gate / (1.0 + jnp.exp(-gate)) * high).astype(BF)
        for c in range(8):
            cols = slice(c * 512, c * 512 + 512)
            pb[e, rows, cols] = dot(hidden, wd[e, :, cols]).astype(BF)

    def experts(e, first, groups):
        def step(i, carry):
            expert(e, first + i)
            return carry

        lax.fori_loop(0, groups, step, 0)

    def landing(t, name):
        i, e, src, n, way = REDUCE[t, name]
        return rb.at[pl.ds(LANDING[t, name], n), :]

    def reduce(t, name):
        i, e, src, n, way = REDUCE[t, name]
        return remote(
            pb.at[e, pl.ds(src, n), :], landing(t, name), r_send.at[i], r_recv.at[i], peer[way]
        )

    def send(t, *names):
        for name in names:
            reduce(t, name).start()

    def landed(t, *names):
        for name in names:
            i, _, _, _, way = REDUCE[t, name]
            ref = landing(t, name)
            remote(ref, ref, r_send.at[i], r_recv.at[i], peer[way]).wait_recv()

    def add_into(t, name, *terms, skip=0):
        _, e, first, _, _ = REDUCE[t, name]
        n = REDUCE[t, terms[0]][3]

        def step(i, carry):
            rows = pl.ds(pl.multiple_of(first + skip + i * 16, 16), 16)
            total = pb[e, rows, :].astype(F32)
            for term in terms:
                start = pl.multiple_of(LANDING[t, term] + i * 16, 16)
                total += rb[pl.ds(start, 16), :].astype(F32)
            pb[e, rows, :] = total.astype(BF)
            return carry

        lax.fori_loop(0, n // 16, step, 0)

    def finish(t, *terms):
        e, off, n, _ = STREAMS[t]
        landed(t, *terms)

        def step(i, carry):
            rows = pl.ds(pl.multiple_of(off + i * 16, 16), 16)
            total = pb[e, rows, :].astype(F32)
            for term in terms:
                start = pl.multiple_of(LANDING[t, term] + i * 16, 16)
                total += rb[pl.ds(start, 16), :].astype(F32)
            total = total.astype(BF)
            for c in range(16):
                place = pl.ds(pl.multiple_of(c * 32 + i * 16, 16), 16)
                stack[t, place, :] = total[:, c * W : c * W + W]
            return carry

        lax.fori_loop(0, n // 16, step, 0)
        fb[t] = dot(there[...], stack[t]).astype(BF)
        go_home(t, True)
        cb[t, block_of(me_p), :] = fb[t, block_of(own_place), :]

    def collect(t):
        came(t, cb, c_recv, me_p)
        rows = dot(back[...], cb[t]).astype(BF)
        for c in range(16):
            rows_in[32 * t : 32 * t + 32, c * W : c * W + W] = rows[32 * c : 32 * c + 32]

    sort_rows(0)
    spread(0, "p", "+o", "-o")
    go_out(2, True)
    sort_rows(1)
    spread(1, "p", "+o", "-o")
    go_out(3, True)
    arrived(0, "+o")
    spread(0, "+f")
    arrived(0, "p")
    spread(0, "+x", "-x")
    arrived(1, "+o")
    spread(1, "+f")
    sort_rows(2)
    spread(2, "p", "+o", "-o")
    arrived(1, "p")
    spread(1, "+x", "-x")
    for copy in weights:
        copy.wait()
    experts(0, 0, 1)
    sort_rows(3)
    spread(3, "+o", "-o", "p")
    lax.fori_loop(0, 16, heads_start, 0)
    arrived(0, "-o", "-x")
    spread(0, "-f")
    arrived(2, "+o")
    spread(2, "+f")
    arrived(2, "p")
    spread(2, "+x", "-x")
    arrived(1, "-o", "-x")
    spread(1, "-f")
    arrived(3, "+o")
    spread(3, "+f", "p-")
    arrived(3, "-o")
    spread(3, "-f", "p+")
    arrived(3, "p")
    experts(1, 0, 1)
    arrived(0, "+x")
    arrived(1, "+x")
    experts(0, 1, 2)
    arrived(2, "-o", "-x")
    spread(2, "-f")
    arrived(3, "+f")
    spread(3, "pl")
    arrived(3, "-f")
    spread(3, "pu")
    arrived(0, "+f", "-f")
    arrived(1, "+f", "-f")
    experts(0, 3, 1)
    send(0, "+2", "-2", "+x", "-x")
    arrived(2, "+x")
    arrived(3, "p-", "p+")
    experts(1, 1, 2)
    lax.fori_loop(0, 16, heads_wait, 0)
    summarize()
    lax.fori_loop(seg + 1, 16, sums_start, 0)
    lax.fori_loop(seg + 1, 16, sums_zero, 0)
    ob[...] = jnp.zeros((1024, 128), BF)
    arrived(2, "+f", "-f")
    arrived(3, "pl", "pu")
    experts(1, 3, 1)
    send(3, "p2", "p+", "p-")
    send(1, "+2", "-2", "+x", "-x")
    send(3, "p")
    landed(0, "+2")
    add_into(0, "+s", "+2")
    send(0, "+s")
    landed(0, "-2")
    add_into(0, "-s", "-2")
    send(0, "-s")
    send(2, "+2", "-2", "+x", "-x")
    for t in range(4):
        go_out(t, False)
    lax.fori_loop(0, 16, heads_sent, 0)
    lax.fori_loop(0, seg, sums_wait, 0)
    lax.fori_loop(0, 12, attend, 0)
    landed(1, "+2")
    add_into(1, "+s", "+2")
    send(1, "+s")
    landed(1, "-2")
    add_into(1, "-s", "-2")
    send(1, "-s")
    landed(0, "+x", "-s")
    add_into(0, "p", "+x", "-s")
    send(0, "p")
    lax.fori_loop(12, 16, attend, 0)
    lax.fori_loop(0, 16, back_start, 0)
    landed(3, "p2")
    add_into(3, "+2", "p2")
    send(3, "+2", "-2")
    landed(2, "+2")
    add_into(2, "+s", "+2")
    send(2, "+s")
    landed(2, "-2")
    add_into(2, "-s", "-2")
    send(2, "-s")
    landed(3, "p+", "p-")
    add_into(3, "+s", "p+")
    add_into(3, "-s", "p-")
    landed(1, "+x", "-s")
    add_into(1, "p", "+x", "-s")
    send(1, "p")
    landed(3, "+2")
    add_into(3, "+s", "+2")
    send(3, "+s")
    landed(3, "-2")
    add_into(3, "-s", "-2", skip=16)
    send(3, "-s")
    finish(0, "+s", "-x", "p")
    landed(2, "+x", "-s")
    add_into(2, "p", "+x", "-s")
    send(2, "p")
    finish(1, "+s", "-x", "p")
    finish(2, "+s", "-x", "p")
    collect(0)
    finish(3, "p", "+s", "-s")
    lax.fori_loop(0, 16, back_wait, 0)
    att_out[...] = ao[...]
    collect(1)
    collect(2)
    for t in range(3):
        go_home(t, False)
    collect(3)
    for c in range(8):
        cols = slice(c * 512, c * 512 + 512)
        mix = dot(share[0], rows_in[:, cols]) + dot(share[1], rows_in[:, cols])
        mix_out[:, cols] = mix.astype(BF)
    go_home(3, False)
    lax.fori_loop(0, 16, back_sent, 0)
    lax.fori_loop(seg + 1, 16, sums_sent, 0)
    for t, name in GATHER:
        gather(t, name).wait_send()
    for t, name in REDUCE:
        reduce(t, name).wait_send()


def on_device(tokens, gain, queries, keys, values, ids, rw, gate, up, down):
    vmem = pl.BlockSpec(memory_space=pltpu.VMEM)
    hbm = pl.BlockSpec(memory_space=pl.ANY)
    dma = pltpu.SemaphoreType.DMA
    head = pltpu.VMEM((1024, 128), BF)
    block = pltpu.VMEM((4, 512, W), BF)
    return pl.pallas_call(
        kernel,
        out_shape=(
            jax.ShapeDtypeStruct((64, 2048), BF),
            jax.ShapeDtypeStruct((64, D), BF),
        ),
        in_specs=[vmem, vmem, hbm, hbm, hbm, vmem, vmem, hbm, hbm, hbm],
        out_specs=(vmem, vmem),
        scratch_shapes=[
            pltpu.VMEM((64, D), BF),
            pltpu.VMEM((512, 512), BF),
            pltpu.VMEM((512, 512), BF),
            block,
            block,
            block,
            pltpu.VMEM((2, 512, D), BF),
            pltpu.VMEM((2, 512, D), BF),
            pltpu.VMEM((2, FFP, D), BF),
            pltpu.VMEM((2, FFP, D), BF),
            pltpu.VMEM((2, FFP, D), BF),
            pltpu.VMEM((LANDING_ROWS, D), BF),
            block,
            block,
            pltpu.VMEM((128, D), BF),
            pltpu.VMEM((2, 64, 128), BF),
            head,
            head,
            head,
            head,
            head,
            head,
            pltpu.VMEM((64, 2048), BF),
            dma((3,)),
            dma((4, 32)),
            dma((4, 32)),
            dma((4, 32)),
            dma((4, 32)),
            dma((len(GATHER),)),
            dma((len(GATHER),)),
            dma((len(REDUCE),)),
            dma((len(REDUCE),)),
            dma((3, 16)),
            dma((3, 16)),
            dma((2, 16)),
            dma((2, 16)),
            dma((16,)),
            dma((16,)),
        ],
        compiler_params=pltpu.CompilerParams(
            collective_id=0, has_side_effects=True, vmem_limit_bytes=60 * 1024 * 1024
        ),
        name="layer",
    )(tokens, gain.reshape(1, D), queries, keys, values, ids.T, rw.T, gate, up, down)


def solution(mesh):
    rows = P(("seq", "exp"), None)
    parts = P("exp", "seq", None)
    return jax.shard_map(
        on_device,
        mesh=mesh,
        in_specs=(rows, P(), rows, rows, rows, rows, rows, parts, parts, parts),
        out_specs=(rows, rows),
        check_vma=False,
    )
```

time: 234 us -> 186 us (0.79); the launches traced: 234 us -> 183 us
  Pallas kernels: 227 us -> 179 us
  local copies, waits for them, and re-layouts: 6.3 us -> 3.54 us
    pallas_call x1, Pallas kernels: 227 us -> 179 us  [on_device(): pl.pallas_call(kernel, out_shape=(jax.ShapeDtypeStruct((64, 2048), BF), j...]
    unnamed x4 -> x2, local copies, waits for them, and re-layouts: 6.3 us -> 3.54 us
where the time goes in v2:
time: 186 us; the launch traced here: 183 us
  Pallas kernels  179 us (96%)
  local copies, waits for them, and re-layouts  3.54 us (2%)
    pallas_call x1, Pallas kernels, on_device(): pl.pallas_call(kernel, out_shape=(jax.ShapeDtypeStruct((64, 2048), BF), j...  179 us

profile of v2, /device:TPU:1, one launch (start us, length us, event | category | flops | bytes accessed | tf_op | source)
XLA Modules:
  0.0 182.8 jit_solution(14931753758596106728)
XLA Ops:
  0.6 178.6 %layer.1 = (bf16[64,2048]{1,0:T(8,128)(2,1)}, bf16[64,4096]{1,0:T(8,128)(2,1)}) custom-call(bf16[64,4096]{1,0:T(8,128)(2,1)} %tok.1, f32[1,4096]{1,0:T(1,128)} %bitcast.3, bf16[64,2048]{1,0:T(8,128)(2,1)} %q.1, bf16[64,2048]{1,0:T(8,128)(2,1)} %k.1, bf16[64,2048]{1,0:T(8,128)(2,1)} %v.1, s32[2,64]{1,0:T(2,128)} %bitcast.4, f32[2,64]{1,0:T(2,128)} %bitcast.5, ...), custom_call_target="tpu_custom_call" | custom-call | tf_op jit(solution)/shard_map/layer/pallas_call | solution.py:647
  179.2 1.7 copy.14
  180.9 1.9 %copy.15 = bf16[64,4096]{1,0:T(8,128)(2,1)} copy(bf16[64,4096]{1,0:T(8,128)(2,1)} %get-tuple-element.5) | data formatting | bytes 1048576
